TPU v7x, 512 devices: a whole 4x4x16 slice. The times are simulated.
512 devices in a mesh: section: 16 (over z), expert: 8 (over y, core), dp: 4 (over x).
Axes of the slice: x: 4, y: 4, z: 16, core: 2. Of those that a mesh axis runs over, the one named last changes fastest.
Arguments:
- tokens: bfloat16 [1024, 3072], P('expert', 'dp'), may hold values from -6 to 6
- expert_ids: int32 [1024, 2], P('expert'), may hold values from 0 to 7, all different within a row; in each aligned block of 128 rows (0 to 127, 128 to 255, ...) at most 64 rows name the same one
- w_gate: bfloat16 [8, 3072, 8192], P('expert', 'dp', 'section'), may hold values from -0.109375 to 0.109375
- w_up: bfloat16 [8, 3072, 8192], P('expert', 'dp', 'section'), may hold values from -0.109375 to 0.109375
- cotangent: bfloat16 [8, 512, 8192], P('expert', None, 'section'), may hold values from -6 to 6
Outputs:
- acted: bfloat16 [8, 512, 8192], P('expert', None, 'section')
- input_grad: bfloat16 [1024, 3072], P('expert', 'dp')
- gate_grad: bfloat16 [8, 3072, 8192], P('expert', 'dp', 'section')
- up_grad: bfloat16 [8, 3072, 8192], P('expert', 'dp', 'section')
Inputs may be any that keep to these rules, and one draw needn't show every extreme that they name: `expert_ids`: each token names two different experts. Among the 128 tokens of one index of the expert axis no expert is named more than 64 times, a bound that some block reaches.
All inputs are finite; a program needn't handle non-finite values.
Results may differ from a plain program's by a relative error of at most 0.0049.
Values may be sent and summed in bfloat16 or wider, within the bound.
A program may use at most 64 MiB of HBM per device.

v0:
```python
import jax
import jax.numpy as jnp
from jax import lax
from jax.sharding import PartitionSpec as P


def local(tokens, expert_ids, w_gate, w_up, cotangent):
    rows, width = tokens.shape
    experts = lax.axis_size("expert")
    capacity = min(rows, 4 * rows // experts)
    wg = w_gate[0]
    wu = w_up[0]
    flat_ids = expert_ids.reshape(-1)
    member = (flat_ids[:, None] == jnp.arange(experts, dtype=jnp.int32)[None, :]).astype(jnp.int32)
    rank = jnp.sum((jnp.cumsum(member, axis=0) - member) * member, axis=1)
    slot = flat_ids * capacity + rank
    token_of = jnp.arange(2 * rows, dtype=jnp.int32) // 2
    source = jnp.full((experts * capacity,), rows, jnp.int32).at[slot].set(token_of)
    occupied = jnp.zeros((experts * capacity,), jnp.bfloat16).at[slot].set(1.0)
    x_pad = jnp.concatenate([tokens, jnp.zeros((1, width), jnp.bfloat16)], axis=0)
    send_x = jnp.take(x_pad, source, axis=0).reshape(experts, capacity, width)
    recv_x, recv_live = (
        lax.all_to_all(send_x, "expert", split_axis=0, concat_axis=0, tiled=True),
        lax.all_to_all(
            occupied.reshape(experts, capacity), "expert", split_axis=0, concat_axis=0, tiled=True
        ),
    )
    x_rows = recv_x.reshape(-1, width)
    parts = (x_rows,)
    part_gate = jnp.dot(parts[0], wg, preferred_element_type=jnp.float32)
    part_up = jnp.dot(parts[0], wu, preferred_element_type=jnp.float32)
    pre_gate, pre_up = lax.psum((part_gate, part_up), "dp")
    sig = jax.nn.sigmoid(pre_gate)
    silu_v = pre_gate * sig
    acted = (silu_v * pre_up).astype(jnp.bfloat16)
    cf = cotangent[0].astype(jnp.float32)
    gate_part = (cf * pre_up * sig * (1.0 + pre_gate * (1.0 - sig))).astype(jnp.bfloat16)
    up_part = (cf * silu_v).astype(jnp.bfloat16)
    contract = (((0,), (0,)), ((), ()))
    gate_grad = lax.dot_general(x_rows, gate_part, contract, preferred_element_type=jnp.float32)
    up_grad = lax.dot_general(x_rows, up_part, contract, preferred_element_type=jnp.float32)
    parts = (gate_part, up_part)
    back = lax.dot_general(
        parts[0], wg, (((1,), (1,)), ((), ())), preferred_element_type=jnp.float32
    ) + lax.dot_general(parts[1], wu, (((1,), (1,)), ((), ())), preferred_element_type=jnp.float32)
    back = (back,)[0]
    whole = lax.psum(back, "section")
    home = lax.all_to_all(
        whole.reshape(experts, capacity, width), "expert", split_axis=0, concat_axis=0, tiled=True
    )
    token_grad = jnp.sum(
        jnp.take(home.reshape(-1, width), slot, axis=0).reshape(rows, 2, width), axis=1
    )
    return (
        acted[None],
        token_grad.astype(jnp.bfloat16),
        gate_grad.astype(jnp.bfloat16)[None],
        up_grad.astype(jnp.bfloat16)[None],
    )


def solution(mesh):
    placed = (
        P("expert", "dp"),
        P("expert", None),
        P("expert", "dp", "section"),
        P("expert", "dp", "section"),
        P("expert", None, "section"),
    )
    return jax.shard_map(
        local,
        mesh=mesh,
        in_specs=placed,
        out_specs=(
            P("expert", None, "section"),
            P("expert", "dp"),
            P("expert", "dp", "section"),
            P("expert", "dp", "section"),
        ),
        check_vma=False,
    )
```

profile of v0, /device:TPU:1, one launch (start us, length us, event | category | flops | bytes accessed | tf_op | source)
XLA Modules:
  0.0 297.3 jit_solution(851770255115678732)
XLA Ops:
  7.2 0.0 copy-start
  7.2 0.0 all-reduce.7.cloned.1.call-start
  7.2 0.7 broadcast_multiply_fusion
  8.0 0.8 copy.14
  8.8 0.1 eq.29
  8.9 0.1 eq.25
  9.0 0.1 copy.13
  9.2 0.1 mul.45
  9.3 0.6 reduce-window.6
  9.9 0.2 slice_reduce_fusion
  10.2 0.1 fusion.16
  10.3 1.4 scatter_custom_fusion
  11.7 0.1 broadcast_in_dim.40
  11.8 0.9 concatenate.3
  12.7 2.0 gather_fusion
  14.8 0.0 copy-start.4
  14.8 0.1 broadcast_select_fusion
  14.9 21.5 %all_to_all.10 = bf16[8,64,768]{2,1,0:T(8,128)(2,1)S(1)} all-to-all(bf16[8,64,768]{2,1,0:T(8,128)(2,1)S(1)} %broadcast_select_fusion), channel_id=1, replica_groups=mesh['section'=16,'expert'=8,'dp'=4] {'expert'}, dimensions={0} | all-to-all | bytes 1572864 | tf_op jit(solution)/shard_map/all_to_all | solution.py:23
  36.4 0.0 copy-done.4
  36.4 1.6 fusion.8
  38.1 0.0 copy-done
  38.1 1.6 fusion.12
  39.6 0.0 copy-start.6
  39.6 0.0 all-reduce.7.cloned.1.call-update
  39.6 0.0 all-reduce.5.cloned.1.call-start
  39.7 73.3 %all-reduce.7.cloned.1.call-done = (f32[512,512]{1,0:T(8,128)}, f32[512,512]{1,0:T(8,128)}) async-done(((f32[512,512]{1,0:T(8,128)}, f32[512,512]{1,0:T(8,128)}), (f32[512,512]{1,0:T(8,128)}, f32[512,512]{1,0:T(8,128)})) %all-reduce.7.cloned.1.call-update) | async-done | bytes 2097168 | tf_op jit(solution)/shard_map/psum | solution.py:32
  113.0 0.0 copy-done.6
  113.0 2.9 fusion.4
  115.9 0.0 copy-start.1
  115.9 0.0 copy-start.2
  115.9 0.0 copy-start.5
  115.9 0.0 copy-start.7
  115.9 0.6 fusion.10
  116.5 0.8 copy-done.2
  117.3 0.2 copy-done.5
  117.5 0.1 copy-done.7
  117.7 1.9 convolution_add_fusion
  119.6 0.0 copy-done.1
  119.6 0.0 all-reduce.5.cloned.1.call-update
  119.6 0.0 copy-start.9
  119.7 132.2 %all-reduce.5.cloned.1.call-done = f32[8,64,768]{2,1,0:T(8,128)} async-done(((f32[8,64,768]{2,1,0:T(8,128)}), f32[8,64,768]{2,1,0:T(8,128)}) %all-reduce.5.cloned.1.call-update) | async-done | bytes 1572880 | tf_op jit(solution)/shard_map/psum | solution.py:47
  251.8 14.7 %all-to-all-start.1 = ((f32[8,64,768]{2,1,0:T(8,128)}), f32[8,64,768]{2,1,0:T(8,128)S(1)}, u32[]{:S(2)}, u32[]{:S(2)}) async-start(f32[8,64,768]{2,1,0:T(8,128)} %all-reduce.5.cloned.1.call-done), calls=%async_computation.1 | async-start | bytes 3145728 | tf_op jit(solution)/shard_map/all_to_all | solution.py:48
  266.5 0.1 reduce_sum.24
  266.7 0.1 copy.16
  266.7 0.0 copy-done.9
  266.7 0.1 copy.17
  266.9 0.0 copy-start.3
  266.9 0.0 copy-start.8
  266.9 2.6 fusion
  269.6 0.0 copy-done.3
  269.6 0.0 copy-done.8
  269.6 1.6 fusion.1
  271.2 15.9 %all-to-all-done.1 = f32[8,64,768]{2,1,0:T(8,128)S(1)} async-done(((f32[8,64,768]{2,1,0:T(8,128)}), f32[8,64,768]{2,1,0:T(8,128)S(1)}, u32[]{:S(2)}, u32[]{:S(2)}) %all-to-all-start.1) | async-done | bytes 1572896 | tf_op jit(solution)/shard_map/all_to_all | solution.py:48
  287.1 1.1 gather_fusion.1
  288.2 0.5 gather.15
  288.7 1.8 select_reduce_fusion
  (10 shorter events, 0.1 us)
Async XLA Ops:
  7.2 30.9 %copy-start = (bf16[1,768,512]{2,1,0:T(8,128)(2,1)S(1)}, bf16[1,768,512]{2,1,0:T(8,128)(2,1)}, u32[]{:S(2)}) copy-start(bf16[1,768,512]{2,1,0:T(8,128)(2,1)} %param.7) | copy-start | bytes 2359300
  7.2 105.8 %all-reduce.7.cloned.1.call-start = ((), (), s32[]{:S(2)}) async-start(), calls=%async_computation.3 | async-start | bytes 4194304 | tf_op jit(solution)/shard_map/psum | solution.py:32
  14.8 21.7 %copy-start.4 = (bf16[1,768,512]{2,1,0:T(8,128)(2,1)S(1)}, bf16[1,768,512]{2,1,0:T(8,128)(2,1)}, u32[]{:S(2)}) copy-start(bf16[1,768,512]{2,1,0:T(8,128)(2,1)} %param.8) | copy-start | bytes 2359300
  39.6 73.4 %copy-start.6 = (bf16[1,512,512]{2,1,0:T(8,128)(2,1)S(1)}, bf16[1,512,512]{2,1,0:T(8,128)(2,1)}, u32[]{:S(2)}) copy-start(bf16[1,512,512]{2,1,0:T(8,128)(2,1)} %param.9) | copy-start | bytes 1572868
  39.6 212.2 %all-reduce.5.cloned.1.call-start = ((), (), s32[]{:S(2)}) async-start(), calls=%async_computation.2 | async-start | bytes 3145728 | tf_op jit(solution)/shard_map/psum | solution.py:47
  115.9 3.7 %copy-start.1 = (bf16[512,512]{1,0:T(8,128)(2,1)}, bf16[512,512]{1,0:T(8,128)(2,1)S(1)}, u32[]{:S(2)}) copy-start(bf16[512,512]{1,0:T(8,128)(2,1)S(1)} %get-tuple-element.6) | copy-start | bytes 1572868
  115.9 1.4 copy-start.2
  115.9 1.6 copy-start.5
  115.9 1.8 copy-start.7
  119.6 147.1 %copy-start.9 = (s32[128,2]{0,1:T(2,128)S(1)}, s32[128,2]{0,1:T(2,128)}, u32[]{:S(2)}) copy-start(s32[128,2]{0,1:T(2,128)} %param.6) | copy-start | bytes 3076
  251.8 35.3 %all-to-all-start.1 = ((f32[8,64,768]{2,1,0:T(8,128)}), f32[8,64,768]{2,1,0:T(8,128)S(1)}, u32[]{:S(2)}, u32[]{:S(2)}) async-start(f32[8,64,768]{2,1,0:T(8,128)} %all-reduce.5.cloned.1.call-done), calls=%async_computation.1 | async-start | bytes 3145728 | tf_op jit(solution)/shard_map/all_to_all | solution.py:48
  266.9 2.7 copy-start.3
  266.9 2.7 copy-start.8
Sparse Core Ops, SparseCore 0:
  39.8 73.2 all-reduce.6
  119.8 132.0 all-reduce.4
where the time goes:
time: 298 us; the launch traced here: 297 us
  waiting for transfers between devices  221 us (74%)
  blocking collectives  21.5 us (7%)
  starting transfers between devices  14.8 us (5%)
  between operations  14.2 us (5%)
  matrix products  9.94 us (3%)
  local copies, waits for them, and re-layouts  9.07 us (3%)
  other arithmetic  6.29 us (2%)
    psum x1, waiting for transfers between devices, local(): whole = lax.psum(back, 'section')  132 us
    psum x1, waiting for transfers between devices, local(): pre_gate, pre_up = lax.psum((part_gate, part_up), 'dp')  73.3 us
    all_to_all x1, blocking collectives, local(): lax.all_to_all(send_x, 'expert', split_axis=0, concat_axis=0, tiled=True)  21.5 us
    all_to_all x1, waiting for transfers between devices, local(): lax.all_to_all(whole.reshape(experts, capacity, width), 'expert', split_a...  15.9 us
    all_to_all x1, starting transfers between devices, local(): lax.all_to_all(whole.reshape(experts, capacity, width), 'expert', split_a...  14.7 us
  transfers between devices with their start and end apart: 3, of which 3 were waited for; matrix products, arithmetic and copies ran while one was open for 2% of the time, Pallas kernels for 0%

commit v1 on v0

--- a/solution.py
+++ b/solution.py
@@ -44,7 +44,9 @@
         parts[0], wg, (((1,), (1,)), ((), ())), preferred_element_type=jnp.float32
     ) + lax.dot_general(parts[1], wu, (((1,), (1,)), ((), ())), preferred_element_type=jnp.float32)
     back = (back,)[0]
-    whole = lax.psum(back, "section")
+    whole = back
+    for hop in (1, 2, 4, 8):
+        whole = whole + lax.ppermute(whole, "section", [(dev, dev ^ hop) for dev in range(16)])
     home = lax.all_to_all(
         whole.reshape(experts, capacity, width), "expert", split_axis=0, concat_axis=0, tiled=True
     )

time: 298 us -> 549 us (1.84)
  the two profiles are of different devices: /device:TPU:1 before, /device:TPU:128 now
where the time goes in v1:
time: 549 us
  waiting for transfers between devices  463 us (84%)
  starting transfers between devices  25.9 us (5%)
  blocking collectives  17.6 us (3%)
  between operations  14.2 us (3%)
  local copies, waits for them, and re-layouts  10.7 us (2%)
  matrix products  8.76 us (2%)
  other arithmetic  8.24 us (2%)
    ppermute x4, waiting for transfers between devices, local(): lax.ppermute(whole, 'section', [(dev, dev ^ hop) for dev in range(16)])  371 us
    psum x1, waiting for transfers between devices, local(): pre_gate, pre_up = lax.psum((part_gate, part_up), 'dp')  75.2 us
    ppermute x4, starting transfers between devices, local(): lax.ppermute(whole, 'section', [(dev, dev ^ hop) for dev in range(16)])  21.5 us
    all_to_all x1, blocking collectives, local(): lax.all_to_all(send_x, 'expert', split_axis=0, concat_axis=0, tiled=True)  17.6 us
    all_to_all x1, waiting for transfers between devices, local(): lax.all_to_all(whole.reshape(experts, capacity, width), 'expert', split_a...  16.9 us
  transfers between devices with their start and end apart: 6, of which 6 were waited for; matrix products, arithmetic and copies ran while one was open for 1% of the time, Pallas kernels for 0%

profile of v1, /device:TPU:128, one launch (start us, length us, event | category | flops | bytes accessed | tf_op | source)
XLA Modules:
  0.0 548.7 jit_solution(16780759255961008246)
XLA Ops:
  7.2 0.0 copy-start
  7.2 0.0 all-reduce.4.cloned.1.call-start
  7.2 0.7 broadcast_multiply_fusion
  8.0 0.8 copy.14
  8.8 0.1 eq.29
  8.9 0.1 eq.25
  9.0 0.1 copy.13
  9.2 0.1 mul.45
  9.3 0.6 reduce-window.6
  9.9 0.2 slice_reduce_fusion
  10.2 0.1 fusion.16
  10.3 1.4 scatter_custom_fusion
  11.7 0.1 broadcast_in_dim.40
  11.8 0.9 concatenate.3
  12.7 2.0 gather_fusion
  14.8 0.0 copy-start.4
  14.8 0.1 broadcast_select_fusion
  14.9 17.6 %all_to_all.10 = bf16[8,64,768]{2,1,0:T(8,128)(2,1)S(1)} all-to-all(bf16[8,64,768]{2,1,0:T(8,128)(2,1)S(1)} %broadcast_select_fusion), channel_id=1, replica_groups=mesh['section'=16,'expert'=8,'dp'=4] {'expert'}, dimensions={0} | all-to-all | bytes 1572864 | tf_op jit(solution)/shard_map/all_to_all | solution.py:23
  32.5 0.0 copy-done.4
  32.5 1.6 fusion.8
  34.1 0.0 copy-done
  34.1 1.6 fusion.12
  35.6 0.0 copy-start.5
  35.6 0.0 all-reduce.4.cloned.1.call-update
  35.7 75.2 %all-reduce.4.cloned.1.call-done = (f32[512,512]{1,0:T(8,128)}, f32[512,512]{1,0:T(8,128)}) async-done(((f32[512,512]{1,0:T(8,128)}, f32[512,512]{1,0:T(8,128)}), (f32[512,512]{1,0:T(8,128)}, f32[512,512]{1,0:T(8,128)})) %all-reduce.4.cloned.1.call-update) | async-done | bytes 2097168 | tf_op jit(solution)/shard_map/psum | solution.py:32
  110.9 0.0 copy-done.5
  110.9 2.9 fusion.4
  113.7 0.0 copy-start.1
  113.8 0.0 copy-start.2
  113.8 0.6 fusion.10
  114.4 0.8 copy-done.2
  115.2 0.8 convolution_add_fusion
  116.0 0.0 copy-done.1
  116.0 3.5 collective-permute-start
  119.5 34.4 %collective-permute-done = f32[512,768]{1,0:T(8,128)S(1)} collective-permute-done((f32[512,768]{1,0:T(8,128)S(1)}, f32[512,768]{1,0:T(8,128)S(1)}, u32[]{:S(2)}, u32[]{:S(2)}) %collective-permute-start) | collective-permute-done | bytes 1572896 | tf_op jit(solution)/shard_map/ppermute | solution.py:49
  153.8 0.2 add.86
  154.0 4.5 collective-permute-start.1
  158.5 67.1 %collective-permute-done.1 = f32[512,768]{1,0:T(8,128)S(1)} collective-permute-done((f32[512,768]{1,0:T(8,128)S(1)}, f32[512,768]{1,0:T(8,128)S(1)}, u32[]{:S(2)}, u32[]{:S(2)}) %collective-permute-start.1) | collective-permute-done | bytes 1572896 | tf_op jit(solution)/shard_map/ppermute | solution.py:49
  225.6 0.2 add.87
  225.8 2.1 collective-permute-start.2
  227.9 167.3 %collective-permute-done.2 = f32[512,768]{1,0:T(8,128)S(1)} collective-permute-done((f32[512,768]{1,0:T(8,128)S(1)}, f32[512,768]{1,0:T(8,128)S(1)}, u32[]{:S(2)}, u32[]{:S(2)}) %collective-permute-start.2) | collective-permute-done | bytes 1572896 | tf_op jit(solution)/shard_map/ppermute | solution.py:49
  395.2 0.2 add.88
  395.4 11.4 %collective-permute-start.3 = (f32[512,768]{1,0:T(8,128)S(1)}, f32[512,768]{1,0:T(8,128)S(1)}, u32[]{:S(2)}, u32[]{:S(2)}) collective-permute-start(f32[512,768]{1,0:T(8,128)S(1)} %add.88), channel_id=1, source_target_pairs={{0,256},{32,288},{64,320},{96,352},{128,384},{160,416},{192,448},{... | collective-permute-start | bytes 4718600 | tf_op jit(solution)/shard_map/ppermute | solution.py:49
  406.8 102.3 %collective-permute-done.3 = f32[512,768]{1,0:T(8,128)S(1)} collective-permute-done((f32[512,768]{1,0:T(8,128)S(1)}, f32[512,768]{1,0:T(8,128)S(1)}, u32[]{:S(2)}, u32[]{:S(2)}) %collective-permute-start.3) | collective-permute-done | bytes 1572896 | tf_op jit(solution)/shard_map/ppermute | solution.py:49
  509.1 1.4 add.89
  510.5 0.0 copy-start.7
  510.5 4.4 all-to-all-start.1
  515.0 0.1 reduce_sum.24
  515.1 0.1 copy.16
  515.2 0.0 copy-done.7
  515.2 0.1 copy.17
  515.3 0.0 copy-start.3
  515.3 0.0 copy-start.6
  515.4 2.6 fusion
  518.0 0.0 copy-done.3
  518.0 0.0 copy-done.6
  518.0 1.6 fusion.1
  519.6 16.9 %all-to-all-done.1 = f32[8,64,768]{2,1,0:T(8,128)S(1)} async-done(((f32[8,64,768]{2,1,0:T(8,128)}), f32[8,64,768]{2,1,0:T(8,128)S(1)}, u32[]{:S(2)}, u32[]{:S(2)}) %all-to-all-start.1) | async-done | bytes 1572896 | tf_op jit(solution)/shard_map/all_to_all | solution.py:50
  536.5 2.0 gather_fusion.1
  538.5 1.6 gather.15
  540.1 1.8 select_reduce_fusion
  (10 shorter events, 0.1 us)
Async XLA Ops:
  7.2 26.9 %copy-start = (bf16[1,768,512]{2,1,0:T(8,128)(2,1)S(1)}, bf16[1,768,512]{2,1,0:T(8,128)(2,1)}, u32[]{:S(2)}) copy-start(bf16[1,768,512]{2,1,0:T(8,128)(2,1)} %param.7) | copy-start | bytes 2359300
  7.2 103.7 %all-reduce.4.cloned.1.call-start = ((), (), s32[]{:S(2)}) async-start(), calls=%async_computation.2 | async-start | bytes 4194304 | tf_op jit(solution)/shard_map/psum | solution.py:32
  14.8 17.7 %copy-start.4 = (bf16[1,768,512]{2,1,0:T(8,128)(2,1)S(1)}, bf16[1,768,512]{2,1,0:T(8,128)(2,1)}, u32[]{:S(2)}) copy-start(bf16[1,768,512]{2,1,0:T(8,128)(2,1)} %param.8) | copy-start | bytes 2359300
  35.6 75.2 %copy-start.5 = (bf16[1,512,512]{2,1,0:T(8,128)(2,1)S(1)}, bf16[1,512,512]{2,1,0:T(8,128)(2,1)}, u32[]{:S(2)}) copy-start(bf16[1,512,512]{2,1,0:T(8,128)(2,1)} %param.9) | copy-start | bytes 1572868
  113.7 2.2 copy-start.1
  113.8 1.4 copy-start.2
  116.0 37.9 %collective-permute-start = (f32[512,768]{1,0:T(8,128)S(1)}, f32[512,768]{1,0:T(8,128)S(1)}, u32[]{:S(2)}, u32[]{:S(2)}) collective-permute-start(f32[512,768]{1,0:T(8,128)S(1)} %convolution_add_fusion), channel_id=1, source_target_pairs={{0,32},{32,0},{64,96},{96,64},{128,160},{160,128},{192,224},{224,1... | collective-permute-start | bytes 4718600 | tf_op jit(solution)/shard_map/ppermute | solution.py:49
  154.0 71.6 %collective-permute-start.1 = (f32[512,768]{1,0:T(8,128)S(1)}, f32[512,768]{1,0:T(8,128)S(1)}, u32[]{:S(2)}, u32[]{:S(2)}) collective-permute-start(f32[512,768]{1,0:T(8,128)S(1)} %add.86), channel_id=1, source_target_pairs={{0,64},{32,96},{64,0},{96,32},{128,192},{160,224},{192,128},{224,1... | collective-permute-start | bytes 4718600 | tf_op jit(solution)/shard_map/ppermute | solution.py:49
  225.8 169.4 %collective-permute-start.2 = (f32[512,768]{1,0:T(8,128)S(1)}, f32[512,768]{1,0:T(8,128)S(1)}, u32[]{:S(2)}, u32[]{:S(2)}) collective-permute-start(f32[512,768]{1,0:T(8,128)S(1)} %add.87), channel_id=1, source_target_pairs={{0,128},{32,160},{64,192},{96,224},{128,0},{160,32},{192,64},{224,... | collective-permute-start | bytes 4718600 | tf_op jit(solution)/shard_map/ppermute | solution.py:49
  395.4 113.8 %collective-permute-start.3 = (f32[512,768]{1,0:T(8,128)S(1)}, f32[512,768]{1,0:T(8,128)S(1)}, u32[]{:S(2)}, u32[]{:S(2)}) collective-permute-start(f32[512,768]{1,0:T(8,128)S(1)} %add.88), channel_id=1, source_target_pairs={{0,256},{32,288},{64,320},{96,352},{128,384},{160,416},{192,448},{... | collective-permute-start | bytes 4718600 | tf_op jit(solution)/shard_map/ppermute | solution.py:49
  510.5 4.6 copy-start.7
  510.5 26.0 %all-to-all-start.1 = ((f32[8,64,768]{2,1,0:T(8,128)}), f32[8,64,768]{2,1,0:T(8,128)S(1)}, u32[]{:S(2)}, u32[]{:S(2)}) async-start(f32[8,64,768]{2,1,0:T(8,128)} %bitcast.48), calls=%async_computation.1 | async-start | bytes 3145728 | tf_op jit(solution)/shard_map/all_to_all | solution.py:50
  515.3 2.7 copy-start.3
  515.3 2.7 copy-start.6
Sparse Core Ops, SparseCore 0:
  35.8 75.0 all-reduce.3
